TPU v7x, 256 devices: a whole 4x4x8 slice. The times are simulated.
256 devices in a mesh: layer: 4 (over y_lo, core), phi: 64 (over y_hi, z, x).
Axes of the slice: x: 4, y: 4 (y_hi: 2, y_lo: 2; y = y_hi * 2 + y_lo), z: 8, core: 2. Of those that a mesh axis runs over, the one named last changes fastest.
Arguments:
- hit_features: bfloat16 [4, 64, 1024, 128], P('layer', 'phi'), may hold values from -6 to 6
- edge_features: bfloat16 [4, 64, 4, 1024, 128], P('layer', 'phi'), may hold values from -6 to 6
- sender_slot: int32 [4, 64, 4, 1024], P('layer', 'phi'), may hold values from 0 to 1023
- receiver_slot: int32 [4, 64, 4, 1024], P('layer', 'phi'), may hold values from 0 to 1023
- edge_count: int32 [4, 64, 4], P('layer', 'phi'), may hold values from 0 to 1024, as said below
- grad_hits: bfloat16 [4, 64, 1024, 128], P('layer', 'phi'), may hold values from -6 to 6
- grad_edges: bfloat16 [4, 64, 4, 1024, 128], P('layer', 'phi'), may hold values from -6 to 6
- w_edge_in: bfloat16 [384, 128], replicated, may hold values from -0.3125 to 0.3125
- w_edge_out: bfloat16 [128, 128], replicated, may hold values from -0.5 to 0.5
- w_node_in: bfloat16 [256, 128], replicated, may hold values from -0.375 to 0.375
- w_node_out: bfloat16 [128, 128], replicated, may hold values from -0.5 to 0.5
Outputs:
- hit_grads: float32 [4, 64, 1024, 128], P('layer', 'phi')
- edge_grads: bfloat16 [4, 64, 4, 1024, 128], P('layer', 'phi')
- edge_in_grad: float32 [384, 128], replicated
- edge_out_grad: float32 [128, 128], replicated
- node_in_grad: float32 [256, 128], replicated
- node_out_grad: float32 [128, 128], replicated
Inputs may be any that keep to these rules, and one draw needn't show every extreme that they name: `edge_count`: live slots come first in each block. Kind 0 edges have their sender in the same shard, kind 1 in the previous layer group, kind 2 in the previous phi sector, kind 3 in the next one (phi closes into a loop). Kind 1 has no live slots in layer group 0. Some block is full in every draw. `sender_slot`: rows of dead slots are arbitrary. `receiver_slot`: rows of dead slots are arbitrary.
All inputs are finite; a program needn't handle non-finite values.
Results may differ from a plain program's by a relative error of at most 0.009.
Values may be sent and summed in bfloat16 or wider, within the bound.
A program may use at most 64 MiB of HBM per device.

v0:
```python
import jax
import jax.numpy as jnp
from jax import lax
from jax.sharding import PartitionSpec as P

norm_eps = 1e-05


def passed_along(value, axis, steps):
    count = lax.axis_size(axis)
    initial, last = (max(0, -steps), min(count, count - steps))
    return lax.ppermute(value, axis, [(source, source + steps) for source in range(initial, last)])


def passed_along_2(block, axis, distance):
    devices = range(lax.axis_size(axis))
    route = [((i - distance) % len(devices), i) for i in devices]
    return lax.ppermute(block, axis, route)


def norm_act(pre_act):
    average = jnp.mean(pre_act, axis=-1, keepdims=True)
    centred = pre_act - average
    spread = jnp.mean(centred * centred, axis=-1, keepdims=True)
    scaled = centred * lax.rsqrt(spread + norm_eps)
    return scaled * jax.nn.sigmoid(scaled)


def norm_act_back(pre_act, upstream):
    _, pullback = jax.vjp(norm_act, pre_act)
    return pullback(upstream)[0]


def one_hot_rows(indices, node_total):
    return (indices[:, None] == lax.iota(jnp.int32, node_total)[None, :]).astype(jnp.bfloat16)


def pick_rows(selector, table):
    return jnp.dot(selector, table, preferred_element_type=jnp.float32)


def split_parts(values):
    upper = values.astype(jnp.bfloat16)
    lower = (values - upper.astype(jnp.float32)).astype(jnp.bfloat16)
    return (upper, lower)


def add_rows(selector, values):
    upper, lower = split_parts(values)
    dims = (((0,), (0,)), ((), ()))
    first = lax.dot_general(selector, upper, dims, preferred_element_type=jnp.float32)
    second = lax.dot_general(selector, lower, dims, preferred_element_type=jnp.float32)
    return first + second


def body(
    hit_features,
    edge_features,
    sender_slot,
    receiver_slot,
    edge_count,
    grad_hits,
    grad_edges,
    w_edge_in,
    w_edge_out,
    w_node_in,
    w_node_out,
):
    local_rows = hit_features[0, 0]
    node_total = local_rows.shape[0]
    features = local_rows.shape[1]
    send_all = sender_slot[0, 0]
    recv_all = receiver_slot[0, 0]
    counts = edge_count[0, 0]
    edge_all = edge_features[0, 0]
    grad_edge_all = grad_edges[0, 0]
    grad_local = grad_hits[0, 0]
    kind_total = send_all.shape[0]
    capacity = send_all.shape[1]
    tile_rows = 256
    tile_total = capacity // tile_rows
    lower_rows = passed_along(local_rows, "layer", 1)
    prev_rows = passed_along_2(local_rows, "phi", 1)
    next_rows = passed_along_2(local_rows, "phi", -1)
    sources = (local_rows, lower_rows, prev_rows, next_rows)
    positions = lax.iota(jnp.int32, capacity)
    live_all = (positions[None, :] < counts[:, None]).astype(jnp.float32)

    def tile_indices(k, offset):
        send_idx = lax.dynamic_slice_in_dim(send_all[k], offset, tile_rows, 0)
        recv_idx = lax.dynamic_slice_in_dim(recv_all[k], offset, tile_rows, 0)
        live_mask = lax.dynamic_slice_in_dim(live_all[k], offset, tile_rows, 0)
        return (send_idx, recv_idx, live_mask)

    def forward_tile(k, offset, send_hot, recv_hot):
        edge_rows = lax.dynamic_slice_in_dim(edge_all[k], offset, tile_rows, 0)
        sender_rows = pick_rows(send_hot, sources[k]).astype(jnp.bfloat16)
        receiver_rows = pick_rows(recv_hot, local_rows).astype(jnp.bfloat16)
        inputs = jnp.concatenate([sender_rows, receiver_rows, edge_rows], axis=-1)
        pre_act = jnp.dot(inputs, w_edge_in, preferred_element_type=jnp.float32)
        hidden = norm_act(pre_act).astype(jnp.bfloat16)
        return (inputs, pre_act, hidden)

    def run_tiles(tile_step, totals):

        def looped(number, inner):
            return tile_step(number * tile_rows, inner)

        return lax.fori_loop(0, tile_total, looped, totals)

    incoming = jnp.zeros((node_total, features), jnp.float32)
    stored = []
    for k in range(kind_total):

        def message_step(offset, totals):
            total, kept = totals
            send_idx, recv_idx, live_mask = tile_indices(k, offset)
            send_hot = one_hot_rows(send_idx, node_total)
            recv_hot = one_hot_rows(recv_idx, node_total)
            inputs, pre_act, hidden = forward_tile(k, offset, send_hot, recv_hot)
            message = (
                jnp.dot(hidden, w_edge_out, preferred_element_type=jnp.float32) * live_mask[:, None]
            )
            total = total + add_rows(recv_hot, message)
            kept = (
                lax.dynamic_update_slice_in_dim(kept[0], inputs, offset, 0),
                lax.dynamic_update_slice_in_dim(kept[1], pre_act, offset, 0),
                lax.dynamic_update_slice_in_dim(kept[2], hidden, offset, 0),
            )
            return (total, kept)

        kept_start = (
            jnp.zeros((capacity, 3 * features), jnp.bfloat16),
            jnp.zeros((capacity, features), jnp.float32),
            jnp.zeros((capacity, features), jnp.bfloat16),
        )
        incoming, kept_done = run_tiles(message_step, (incoming, kept_start))
        stored.append(kept_done)
    incoming = incoming.astype(jnp.bfloat16)
    node_in = jnp.concatenate([local_rows, incoming], axis=-1)
    node_pre = jnp.dot(node_in, w_node_in, preferred_element_type=jnp.float32)
    node_hidden = norm_act(node_pre).astype(jnp.bfloat16)
    node_hidden_grad = jnp.dot(grad_local, w_node_out.T, preferred_element_type=jnp.float32)
    node_out_part = jnp.dot(node_hidden.T, grad_local, preferred_element_type=jnp.float32)
    node_pre_grad = norm_act_back(node_pre, node_hidden_grad).astype(jnp.bfloat16)
    node_input_grad = jnp.dot(node_pre_grad, w_node_in.T, preferred_element_type=jnp.float32)
    node_in_part = jnp.dot(node_in.T, node_pre_grad, preferred_element_type=jnp.float32)
    incoming_upper, incoming_lower = split_parts(node_input_grad[:, features:])
    recv_total = jnp.zeros((node_total, features), jnp.float32)
    in_total = jnp.zeros((3 * features, features), jnp.float32)
    out_total = jnp.zeros((features, features), jnp.float32)
    send_parts = []
    edge_parts = []
    for k in range(kind_total):

        def back_step(offset, totals):
            recv_sum, send_sum, in_sum, out_sum, edge_done = totals
            send_idx, recv_idx, live_mask = tile_indices(k, offset)
            send_hot = one_hot_rows(send_idx, node_total)
            recv_hot = one_hot_rows(recv_idx, node_total)
            inputs = lax.dynamic_slice_in_dim(stored[k][0], offset, tile_rows, 0)
            pre_act = lax.dynamic_slice_in_dim(stored[k][1], offset, tile_rows, 0)
            hidden = lax.dynamic_slice_in_dim(stored[k][2], offset, tile_rows, 0)
            grad_rows = lax.dynamic_slice_in_dim(grad_edge_all[k], offset, tile_rows, 0)
            picked = pick_rows(recv_hot, incoming_upper) + pick_rows(recv_hot, incoming_lower)
            message_grad = (live_mask[:, None] * (grad_rows.astype(jnp.float32) + picked)).astype(
                jnp.bfloat16
            )
            hidden_grad = jnp.dot(message_grad, w_edge_out.T, preferred_element_type=jnp.float32)
            pre_grad = norm_act_back(pre_act, hidden_grad).astype(jnp.bfloat16)
            input_grad = jnp.dot(pre_grad, w_edge_in.T, preferred_element_type=jnp.float32)
            edge_new = (grad_rows.astype(jnp.float32) + input_grad[:, 2 * features :]).astype(
                jnp.bfloat16
            )
            edge_done = lax.dynamic_update_slice_in_dim(edge_done, edge_new, offset, 0)
            recv_sum = recv_sum + add_rows(recv_hot, input_grad[:, features : 2 * features])
            send_sum = send_sum + add_rows(send_hot, input_grad[:, :features])
            in_sum = in_sum + jnp.dot(inputs.T, pre_grad, preferred_element_type=jnp.float32)
            out_sum = out_sum + jnp.dot(hidden.T, message_grad, preferred_element_type=jnp.float32)
            return (recv_sum, send_sum, in_sum, out_sum, edge_done)

        start_totals = (
            recv_total,
            jnp.zeros((node_total, features), jnp.float32),
            in_total,
            out_total,
            grad_edge_all[k],
        )
        recv_total, send_sum, in_total, out_total, edge_done = run_tiles(back_step, start_totals)
        send_parts.append(send_sum)
        edge_parts.append(edge_done)
    from_upper = passed_along(send_parts[1].astype(jnp.bfloat16), "layer", -1).astype(jnp.float32)
    from_next = passed_along_2(send_parts[2].astype(jnp.bfloat16), "phi", -1).astype(jnp.float32)
    from_prev = passed_along_2(send_parts[3].astype(jnp.bfloat16), "phi", 1).astype(jnp.float32)
    returned = from_next + from_prev
    hit_total = (
        grad_local.astype(jnp.float32)
        + node_input_grad[:, :features]
        + recv_total
        + send_parts[0]
        + from_upper
        + returned
    )
    summed = lax.psum((in_total, out_total, node_in_part, node_out_part), ("layer", "phi"))
    shard_count = lax.axis_size("layer") * lax.axis_size("phi")
    edge_stack = jnp.stack(edge_parts)
    return (
        hit_total[None, None],
        edge_stack[None, None],
        summed[0] / shard_count,
        summed[1] / shard_count,
        summed[2] / shard_count,
        summed[3] / shard_count,
    )


def solution(mesh):
    placed = (
        P("layer", "phi", None, None),
        P("layer", "phi", None, None, None),
        P("layer", "phi", None, None),
        P("layer", "phi", None, None),
        P("layer", "phi", None),
        P("layer", "phi", None, None),
        P("layer", "phi", None, None, None),
        P(),
        P(),
        P(),
        P(),
    )
    return jax.shard_map(
        body,
        mesh=mesh,
        in_specs=placed,
        out_specs=(
            P("layer", "phi", None, None),
            P("layer", "phi", None, None, None),
            P(),
            P(),
            P(),
            P(),
        ),
        check_vma=False,
    )
```

profile of v0, /device:TPU:2, one launch (start us, length us, event | category | flops | bytes accessed | tf_op | source)
XLA Modules:
  0.0 593.0 jit_solution(756839716940063795)
XLA Ops:
  7.2 2.4 collective-permute-start
  16.6 33.2 %while.168 = (s32[]{:T(128)}, f32[1024,128]{1,0:T(8,128)S(1)}, bf16[1024,384]{0,1:T(8,128)(2,1)}, f32[1024,128]{0,1:T(8,128)}, bf16[1024,128]{0,1:T(8,128)(2,1)S...) while((s32[]{:T(128)}, f32[1024,128]{1,0:T(8,128)S(1)}, ...), condition=%wide.region_3.0_spmd.clone, body=%wide.region_0.0_spmd.clone.sunk | while | flops 305463552 | bytes 8575457 | solution.py:109
  54.2 26.9 %while.165 = (s32[]{:T(128)}, f32[1024,128]{1,0:T(8,128)S(1)}, bf16[1024,384]{0,1:T(8,128)(2,1)}, f32[1024,128]{0,1:T(8,128)}, bf16[1024,128]{0,1:T(8,128)(2,1)}...) while((s32[]{:T(128)}, f32[1024,128]{1,0:T(8,128)S(1)}, ...), condition=%wide.region_7.0_spmd, body=%wide.region_4.0_spmd.sunk | while | flops 305332480 | bytes 5421311 | solution.py:109
  83.7 27.0 %while.166 = (s32[]{:T(128)}, f32[1024,128]{1,0:T(8,128)S(1)}, bf16[1024,384]{0,1:T(8,128)(2,1)}, f32[1024,128]{0,1:T(8,128)}, bf16[1024,128]{0,1:T(8,128)(2,1)}...) while((s32[]{:T(128)}, f32[1024,128]{1,0:T(8,128)S(1)}, ...), condition=%wide.region_11.0_spmd, body=%wide.region_8.0_spmd.sunk | while | flops 305332480 | bytes 5421311 | solution.py:109
  113.3 27.0 %while.167 = (s32[]{:T(128)}, f32[1024,128]{1,0:T(8,128)S(1)}, bf16[1024,384]{0,1:T(8,128)(2,1)}, f32[1024,128]{0,1:T(8,128)}, bf16[1024,128]{0,1:T(8,128)(2,1)}...) while((s32[]{:T(128)}, f32[1024,128]{1,0:T(8,128)S(1)}, ...), condition=%wide.region_15.0_spmd, body=%wide.region_12.0_spmd.sunk | while | flops 305332480 | bytes 5421311 | solution.py:109
  144.1 1.9 fusion.147
  148.2 51.9 %while.169 = (s32[]{:T(128)}, f32[1024,128]{1,0:T(8,128)S(1)}, f32[1024,128]{1,0:T(8,128)}, f32[384,128]{1,0:T(8,128)S(1)}, f32[128,128]{1,0:T(8,128)S(1)}, /*in...) while((s32[]{:T(128)}, f32[1024,128]{1,0:T(8,128)S(1)}, ...), condition=%wide.region_25.26_spmd.clone, body=%wide.region_20.25_spmd.clone.sunk | while | flops 473990912 | bytes 11069784 | solution.py:109
  167.1 2.4 fusion.376
  180.4 2.4 fusion.376
  193.6 2.4 fusion.376
  200.1 40.0 %while.170 = (s32[]{:T(128)}, f32[1024,128]{1,0:T(8,128)S(1)}, f32[1024,128]{1,0:T(8,128)}, f32[384,128]{1,0:T(8,128)S(1)}, f32[128,128]{1,0:T(8,128)S(1)}, /*in...) while((s32[]{:T(128)}, f32[1024,128]{1,0:T(8,128)S(1)}, ...), condition=%wide.region_31.0_spmd.clone, body=%wide.region_26.31_spmd.clone.sunk | while | flops 473794304 | bytes 13166961 | solution.py:109
  213.1 2.4 fusion.394
  223.4 2.4 fusion.394
  233.6 2.4 fusion.394
  240.1 39.9 %while.171 = (s32[]{:T(128)}, f32[1024,128]{1,0:T(8,128)S(1)}, f32[1024,128]{1,0:T(8,128)}, f32[384,128]{1,0:T(8,128)S(1)}, f32[128,128]{1,0:T(8,128)S(1)}, /*in...) while((s32[]{:T(128)}, f32[1024,128]{1,0:T(8,128)S(1)}, ...), condition=%wide.region_37.38_spmd.clone, body=%wide.region_32.37_spmd.clone.sunk | while | flops 473794304 | bytes 13166961 | solution.py:109
  253.1 2.4 fusion.412
  263.3 2.4 fusion.412
  273.6 2.4 fusion.412
  280.1 39.9 %while.172 = (s32[]{:T(128)}, f32[1024,128]{1,0:T(8,128)S(1)}, f32[1024,128]{1,0:T(8,128)}, f32[384,128]{1,0:T(8,128)S(1)}, f32[128,128]{1,0:T(8,128)S(1)}, /*in...) while((s32[]{:T(128)}, f32[1024,128]{1,0:T(8,128)S(1)}, ...), condition=%wide.region_43.44_spmd.clone, body=%wide.region_38.43_spmd.clone.sunk | while | flops 473794304 | bytes 13166961 | solution.py:109
  293.0 2.4 fusion.430
  303.2 2.4 fusion.430
  313.5 2.4 fusion.430
  324.7 7.7 %collective-permute-start.4 = (bf16[1024,128]{1,0:T(8,128)(2,1)}, bf16[1024,128]{1,0:T(8,128)(2,1)S(1)}, u32[]{:S(2)}, u32[]{:S(2)}) collective-permute-start(bf16[1024,128]{1,0:T(8,128)(2,1)} %convert_element_type.563), channel_id=1, source_target_pairs={{1,0},{2,1},{3,2},{4,3},{5,4},{6,5},{7,6},{8,7},{9,8},{10,9},{11,1... | collective-permute-start | bytes 786440 | tf_op jit(solution)/shard_map/ppermute | solution.py:18
  335.6 244.9 %all-reduce.3.cloned.1.call-done = (f32[384,128]{1,0:T(8,128)}, f32[128,128]{1,0:T(8,128)}, f32[256,128]{1,0:T(8,128)}, f32[128,128]{1,0:T(8,128)}) async-done(((f32[384,128]{1,0:T(8,128)}, f32[128,128]{1,0:T(8,128)}, f32[256,128]{1,0:T(8,128)}, f32[128,128]{1,0:T(8,128)}), (f32[384,128]{1,0:T(8,128)}, f32[128,128]{1,0:T(8,128)}, f32[256,128]{1,0:T(8,128)}, ...) | async-done | bytes 458768 | tf_op jit(solution)/shard_map/psum | solution.py:204
  (946 shorter events, 288.8 us)
Async XLA Ops:
  7.2 133.1 %copy-start = (bf16[256,128]{1,0:T(8,128)(2,1)S(1)}, bf16[256,128]{1,0:T(8,128)(2,1)}, u32[]{:S(2)}) copy-start(bf16[256,128]{1,0:T(8,128)(2,1)} %param.36) | copy-start | bytes 196612
  7.2 573.2 %all-reduce.3.cloned.1.call-start = ((), (), s32[]{:S(2)}) async-start(), calls=%async_computation | async-start | bytes 917504 | tf_op jit(solution)/shard_map/psum | solution.py:204
  7.2 44.3 %collective-permute-start = (bf16[1024,128]{1,0:T(8,128)(2,1)}, bf16[1024,128]{1,0:T(8,128)(2,1)}, u32[]{:S(2)}, u32[]{:S(2)}) collective-permute-start(bf16[1024,128]{1,0:T(8,128)(2,1)} %bitcast.13), channel_id=1, source_target_pairs={{0,64},{64,128},{128,192},{1,65},{65,129},{129,193},{2,66},{66,130... | collective-permute-start | bytes 786440 | tf_op jit(solution)/shard_map/ppermute | solution.py:12
  9.7 71.4 %collective-permute-start.1 = (bf16[1024,128]{1,0:T(8,128)(2,1)}, bf16[1024,128]{1,0:T(8,128)(2,1)}, u32[]{:S(2)}, u32[]{:S(2)}) collective-permute-start(bf16[1024,128]{1,0:T(8,128)(2,1)} %bitcast.13), channel_id=1, source_target_pairs={{63,0},{0,1},{1,2},{2,3},{3,4},{4,5},{5,6},{6,7},{7,8},{8,9},{9,10... | collective-permute-start | bytes 786440 | tf_op jit(solution)/shard_map/ppermute | solution.py:18
  11.2 99.5 %collective-permute-start.2 = (bf16[1024,128]{1,0:T(8,128)(2,1)}, bf16[1024,128]{1,0:T(8,128)(2,1)}, u32[]{:S(2)}, u32[]{:S(2)}) collective-permute-start(bf16[1024,128]{1,0:T(8,128)(2,1)} %bitcast.13), channel_id=1, source_target_pairs={{1,0},{2,1},{3,2},{4,3},{5,4},{6,5},{7,6},{8,7},{9,8},{10,9},{11,1... | collective-permute-start | bytes 786440 | tf_op jit(solution)/shard_map/ppermute | solution.py:18
  16.6 33.9 %copy-start.3 = (bf16[1,1,4,1024,128]{4,3,2,1,0:T(8,128)(2,1)S(1)}, bf16[1,1,4,1024,128]{4,3,2,1,0:T(8,128)(2,1)}, u32[]{:S(2)}) copy-start(bf16[1,1,4,1024,128]{4,3,2,1,0:T(8,128)(2,1)} %param.33) | copy-start | bytes 3145732
  16.7 5.4 copy-start.37
  25.0 5.4 copy-start.37
  33.3 5.4 copy-start.37
  41.6 5.4 copy-start.37
  219.6 1.5 copy-start.31
  240.1 1.5 copy-start.33
  320.0 3.9 copy-start.6
  322.4 9.9 %copy-start.7 = (f32[1024,128]{1,0:T(8,128)S(1)}, f32[1024,128]{1,0:T(8,128)}, u32[]{:S(2)}) copy-start(f32[1024,128]{1,0:T(8,128)} %get-tuple-element.1998) | copy-start | bytes 1572868
  322.4 262.7 %collective-permute-start.5 = (bf16[1024,128]{1,0:T(8,128)(2,1)}, bf16[1024,128]{1,0:T(8,128)(2,1)S(1)}, u32[]{:S(2)}, u32[]{:S(2)}) collective-permute-start(bf16[1024,128]{1,0:T(8,128)(2,1)} %convert_element_type.565), channel_id=1, source_target_pairs={{63,0},{0,1},{1,2},{2,3},{3,4},{4,5},{5,6},{6,7},{7,8},{8,9},{9,10... | collective-permute-start | bytes 786440 | tf_op jit(solution)/shard_map/ppermute | solution.py:18
  323.9 10.5 %copy-start.26 = (bf16[1024,128]{1,0:T(8,128)(2,1)S(1)}, bf16[1024,128]{1,0:T(8,128)(2,1)}, u32[]{:S(2)}) copy-start(bf16[1024,128]{1,0:T(8,128)(2,1)} %get-tuple-element.2001) | copy-start | bytes 786436
  324.7 260.5 %collective-permute-start.4 = (bf16[1024,128]{1,0:T(8,128)(2,1)}, bf16[1024,128]{1,0:T(8,128)(2,1)S(1)}, u32[]{:S(2)}, u32[]{:S(2)}) collective-permute-start(bf16[1024,128]{1,0:T(8,128)(2,1)} %convert_element_type.563), channel_id=1, source_target_pairs={{1,0},{2,1},{3,2},{4,3},{5,4},{6,5},{7,6},{8,7},{9,8},{10,9},{11,1... | collective-permute-start | bytes 786440 | tf_op jit(solution)/shard_map/ppermute | solution.py:18
  332.4 2.0 copy-start.23
  332.4 2.0 copy-start.24
  332.4 2.1 copy-start.25
  333.1 252.1 %collective-permute-start.3 = (bf16[1024,128]{1,0:T(8,128)(2,1)}, bf16[1024,128]{1,0:T(8,128)(2,1)S(1)}, u32[]{:S(2)}, u32[]{:S(2)}) collective-permute-start(bf16[1024,128]{1,0:T(8,128)(2,1)} %convert_element_type.561), channel_id=1, source_target_pairs={{64,0},{128,64},{192,128},{65,1},{129,65},{193,129},{66,2},{130,66... | collective-permute-start | bytes 786440 | tf_op jit(solution)/shard_map/ppermute | solution.py:12
  334.4 250.7 %copy-start.13 = (f32[1024,256]{1,0:T(8,128)S(1)}, f32[1024,256]{1,0:T(8,128)}, u32[]{:S(2)}) copy-start(f32[1024,256]{1,0:T(8,128)} %copy-done.12) | copy-start | bytes 3145732
  335.6 249.6 %copy-start.8 = (f32[1024,128]{1,0:T(8,128)S(1)}, f32[1024,128]{1,0:T(8,128)}, u32[]{:S(2)}) copy-start(f32[1024,128]{1,0:T(8,128)} %get-tuple-element.1997) | copy-start | bytes 1572868
  583.5 1.7 copy-start.28
  (98 other events, 96.8 us)
Sparse Core Ops, SparseCore 0:
  320.8 259.5 all-reduce.2
where the time goes:
time: 598 us; the launch traced here: 593 us
  waiting for transfers between devices  245 us (41%)
  matrix products  212 us (35%)
  other arithmetic  66.8 us (11%)
  local copies, waits for them, and re-layouts  36.3 us (6%)
  starting transfers between devices  15 us (3%)
  between operations  14.3 us (2%)
    psum x1, waiting for transfers between devices, body(): lax.psum((in_total, out_total, node_in_part, node_out_part), ('layer', 'p...  245 us
    dot_general x64, matrix products, pick_rows(): return jnp.dot(selector, table, preferred_element_type=jnp.float32)  71.2 us
    dot_general x48, matrix products, add_rows(): lax.dot_general(selector, lower, dims, preferred_element_type=jnp.float32)  55.7 us
    dot_general x48, matrix products, add_rows(): lax.dot_general(selector, upper, dims, preferred_element_type=jnp.float32)  26.7 us
    dot_general x16, matrix products, back_step(): jnp.dot(inputs.T, pre_grad, preferred_element_type=jnp.float32)  18.4 us
    while x184, local copies, waits for them, and re-layouts  17.3 us
    dot_general x16, matrix products, back_step(): jnp.dot(hidden.T, message_grad, preferred_element_type=jnp.float32)  16.4 us
  transfers between devices with their start and end apart: 7, of which 1 were waited for; matrix products, arithmetic and copies ran while one was open for 16% of the time, Pallas kernels for 0%

commit v1 on v0

--- a/solution.py
+++ b/solution.py
@@ -1,9 +1,17 @@
+import functools
 import jax
 import jax.numpy as jnp
 from jax import lax
 from jax.sharding import PartitionSpec as P
 
 norm_eps = 1e-05
+
+
+def boxes_open(v0, along_axis, net_axis):
+    return lax.psum(lax.psum(v0, along_axis), net_axis)
+
+
+list_patches_on = functools.partial(boxes_open, along_axis="layer", net_axis="phi")
 
 
 def passed_along(value, axis, steps):
@@ -201,7 +209,7 @@
         + from_upper
         + returned
     )
-    summed = lax.psum((in_total, out_total, node_in_part, node_out_part), ("layer", "phi"))
+    summed = list_patches_on((in_total, out_total, node_in_part, node_out_part))
     shard_count = lax.axis_size("layer") * lax.axis_size("phi")
     edge_stack = jnp.stack(edge_parts)
     return (

time: 598 us -> 1090 us (1.82)
  waiting for transfers between devices: 245 us -> 720 us
  local copies, waits for them, and re-layouts: 36.3 us -> 66.5 us
  matrix products: 212 us -> 190 us
    psum x1 -> x2, waiting for transfers between devices: 245 us -> 720 us  [boxes_open(): return lax.psum(lax.psum(v0, along_axis), net_axis)]
    while x184 -> x376, local copies, waits for them, and re-layouts: 17.3 us -> 47.2 us
    dot_general x64, matrix products: 71.2 us -> 47.4 us  [pick_rows(): return jnp.dot(selector, table, preferred_element_type=jnp.float32)]
  transfers between devices with their start and end apart: 7 -> 8, of which waited for: 1 -> 2; matrix products, arithmetic and copies ran while one was open for 16% -> 9% of each run, Pallas kernels for 0% -> 0%
where the time goes in v1:
time: 1090 us; the launch traced here: 1080 us
  waiting for transfers between devices  720 us (66%)
  matrix products  190 us (17%)
  other arithmetic  69 us (6%)
  local copies, waits for them, and re-layouts  66.5 us (6%)
  starting transfers between devices  15.2 us (1%)
  between operations  14.3 us (1%)
    psum x2, waiting for transfers between devices, boxes_open(): return lax.psum(lax.psum(v0, along_axis), net_axis)  720 us
    dot_general x48, matrix products, add_rows(): lax.dot_general(selector, lower, dims, preferred_element_type=jnp.float32)  59.6 us
    dot_general x64, matrix products, pick_rows(): return jnp.dot(selector, table, preferred_element_type=jnp.float32)  47.4 us
    while x376, local copies, waits for them, and re-layouts  47.2 us
    dot_general x48, matrix products, add_rows(): lax.dot_general(selector, upper, dims, preferred_element_type=jnp.float32)  26.7 us
  transfers between devices with their start and end apart: 8, of which 2 were waited for; matrix products, arithmetic and copies ran while one was open for 9% of the time, Pallas kernels for 0%

profile of v1, /device:TPU:2, one launch (start us, length us, event | category | flops | bytes accessed | tf_op | source)
XLA Modules:
  0.0 1079.4 jit_solution(3383421439632286404)
XLA Ops:
  7.2 2.5 collective-permute-start
  16.7 31.7 %while.168 = (s32[]{:T(128)}, f32[1024,128]{1,0:T(8,128)S(1)}, bf16[1024,384]{0,1:T(8,128)(2,1)}, f32[1024,128]{0,1:T(8,128)}, bf16[1024,128]{0,1:T(8,128)(2,1)}...) while((s32[]{:T(128)}, f32[1024,128]{1,0:T(8,128)S(1)}, ...), condition=%wide.region_3.0_spmd.clone, body=%wide.region_0.0_spmd.clone.sunk | while | flops 305463552 | bytes 8051185 | solution.py:117
  52.1 27.0 %while.165 = (s32[]{:T(128)}, f32[1024,128]{1,0:T(8,128)S(1)}, bf16[1024,384]{0,1:T(8,128)(2,1)}, f32[1024,128]{0,1:T(8,128)}, bf16[1024,128]{0,1:T(8,128)(2,1)}...) while((s32[]{:T(128)}, f32[1024,128]{1,0:T(8,128)S(1)}, ...), condition=%wide.region_7.0_spmd, body=%wide.region_4.0_spmd.sunk | while | flops 305332480 | bytes 5421311 | solution.py:117
  81.7 27.0 %while.166 = (s32[]{:T(128)}, f32[1024,128]{1,0:T(8,128)S(1)}, bf16[1024,384]{0,1:T(8,128)(2,1)}, f32[1024,128]{0,1:T(8,128)}, bf16[1024,128]{0,1:T(8,128)(2,1)}...) while((s32[]{:T(128)}, f32[1024,128]{1,0:T(8,128)S(1)}, ...), condition=%wide.region_11.0_spmd, body=%wide.region_8.0_spmd.sunk | while | flops 305332480 | bytes 5421311 | solution.py:117
  111.3 27.0 %while.167 = (s32[]{:T(128)}, f32[1024,128]{1,0:T(8,128)S(1)}, bf16[1024,384]{0,1:T(8,128)(2,1)}, f32[1024,128]{0,1:T(8,128)}, bf16[1024,128]{0,1:T(8,128)(2,1)}...) while((s32[]{:T(128)}, f32[1024,128]{1,0:T(8,128)S(1)}, ...), condition=%wide.region_15.0_spmd, body=%wide.region_12.0_spmd.sunk | while | flops 305332480 | bytes 5421311 | solution.py:117
  144.5 55.4 %while.169 = (s32[]{:T(128)}, f32[1024,128]{1,0:T(8,128)S(1)}, f32[1024,128]{1,0:T(8,128)}, f32[384,128]{1,0:T(8,128)S(1)}, f32[128,128]{1,0:T(8,128)S(1)}, /*in...) while((s32[]{:T(128)}, f32[1024,128]{1,0:T(8,128)S(1)}, ...), condition=%wide.region_25.26_spmd.clone, body=%wide.region_20.25_spmd.clone.sunk | while | flops 473990912 | bytes 12265984 | solution.py:117
  165.1 2.4 fusion.376
  179.2 2.4 fusion.376
  193.3 2.4 fusion.376
  199.9 43.7 %while.170 = (s32[]{:T(128)}, f32[1024,128]{1,0:T(8,128)S(1)}, f32[1024,128]{1,0:T(8,128)}, f32[384,128]{1,0:T(8,128)S(1)}, f32[128,128]{1,0:T(8,128)S(1)}, /*in...) while((s32[]{:T(128)}, f32[1024,128]{1,0:T(8,128)S(1)}, ...), condition=%wide.region_31.0_spmd.clone, body=%wide.region_26.31_spmd.clone.sunk | while | flops 473794304 | bytes 14363161 | solution.py:117
  214.7 2.4 fusion.394
  225.9 2.4 fusion.394
  237.1 2.4 fusion.394
  243.6 43.7 %while.171 = (s32[]{:T(128)}, f32[1024,128]{1,0:T(8,128)S(1)}, f32[1024,128]{1,0:T(8,128)}, f32[384,128]{1,0:T(8,128)S(1)}, f32[128,128]{1,0:T(8,128)S(1)}, /*in...) while((s32[]{:T(128)}, f32[1024,128]{1,0:T(8,128)S(1)}, ...), condition=%wide.region_37.38_spmd.clone, body=%wide.region_32.37_spmd.clone.sunk | while | flops 473794304 | bytes 14363161 | solution.py:117
  258.4 2.4 fusion.412
  269.6 2.4 fusion.412
  280.8 2.4 fusion.412
  287.3 43.7 %while.172 = (s32[]{:T(128)}, f32[1024,128]{1,0:T(8,128)S(1)}, f32[1024,128]{1,0:T(8,128)}, f32[384,128]{1,0:T(8,128)S(1)}, f32[128,128]{1,0:T(8,128)S(1)}, /*in...) while((s32[]{:T(128)}, f32[1024,128]{1,0:T(8,128)S(1)}, ...), condition=%wide.region_43.44_spmd.clone, body=%wide.region_38.43_spmd.clone.sunk | while | flops 473794304 | bytes 14363161 | solution.py:117
  302.1 2.4 fusion.430
  313.2 2.4 fusion.430
  324.4 2.4 fusion.430
  335.7 7.7 collective-permute-start.4
  345.6 36.2 %all-reduce.7.cloned.1.call-done = (f32[384,128]{1,0:T(8,128)}, f32[128,128]{1,0:T(8,128)}, f32[256,128]{1,0:T(8,128)}, f32[128,128]{1,0:T(8,128)}) async-done(((f32[384,128]{1,0:T(8,128)}, f32[128,128]{1,0:T(8,128)}, f32[256,128]{1,0:T(8,128)}, f32[128,128]{1,0:T(8,128)}), (f32[384,128]{1,0:T(8,128)}, f32[128,128]{1,0:T(8,128)}, f32[256,128]{1,0:T(8,128)}, ...) | async-done | bytes 458768 | tf_op jit(solution)/shard_map/psum | solution.py:11
  385.7 683.6 %all-reduce.5.cloned.1.call-done = (f32[384,128]{1,0:T(8,128)}, f32[128,128]{1,0:T(8,128)}, f32[256,128]{1,0:T(8,128)}, f32[128,128]{1,0:T(8,128)}) async-done(((f32[384,128]{1,0:T(8,128)}, f32[128,128]{1,0:T(8,128)}, f32[256,128]{1,0:T(8,128)}, f32[128,128]{1,0:T(8,128)}), (f32[384,128]{1,0:T(8,128)}, f32[128,128]{1,0:T(8,128)}, f32[256,128]{1,0:T(8,128)}, ...) | async-done | bytes 458768 | tf_op jit(solution)/shard_map/psum | solution.py:11
  (1149 shorter events, 301.4 us)
Async XLA Ops:
  7.2 131.1 %copy-start = (bf16[256,128]{1,0:T(8,128)(2,1)S(1)}, bf16[256,128]{1,0:T(8,128)(2,1)}, u32[]{:S(2)}) copy-start(bf16[256,128]{1,0:T(8,128)(2,1)} %param.36) | copy-start | bytes 196612
  7.2 374.6 %all-reduce.7.cloned.1.call-start = ((), (), s32[]{:S(2)}) async-start(), calls=%async_computation.1 | async-start | bytes 917504 | tf_op jit(solution)/shard_map/psum | solution.py:11
  7.2 42.2 %collective-permute-start = (bf16[1024,128]{1,0:T(8,128)(2,1)}, bf16[1024,128]{1,0:T(8,128)(2,1)}, u32[]{:S(2)}, u32[]{:S(2)}) collective-permute-start(bf16[1024,128]{1,0:T(8,128)(2,1)} %bitcast.285), channel_id=1, source_target_pairs={{0,64},{64,128},{128,192},{1,65},{65,129},{129,193},{2,66},{66,130... | collective-permute-start | bytes 786440 | tf_op jit(solution)/shard_map/ppermute | solution.py:20
  9.7 69.4 %collective-permute-start.1 = (bf16[1024,128]{1,0:T(8,128)(2,1)}, bf16[1024,128]{1,0:T(8,128)(2,1)}, u32[]{:S(2)}, u32[]{:S(2)}) collective-permute-start(bf16[1024,128]{1,0:T(8,128)(2,1)} %bitcast.286), channel_id=1, source_target_pairs={{63,0},{0,1},{1,2},{2,3},{3,4},{4,5},{5,6},{6,7},{7,8},{8,9},{9,10... | collective-permute-start | bytes 786440 | tf_op jit(solution)/shard_map/ppermute | solution.py:26
  11.2 97.6 %collective-permute-start.2 = (bf16[1024,128]{1,0:T(8,128)(2,1)}, bf16[1024,128]{1,0:T(8,128)(2,1)}, u32[]{:S(2)}, u32[]{:S(2)}) collective-permute-start(bf16[1024,128]{1,0:T(8,128)(2,1)} %bitcast.287), channel_id=1, source_target_pairs={{1,0},{2,1},{3,2},{4,3},{5,4},{6,5},{7,6},{8,7},{9,8},{10,9},{11,1... | collective-permute-start | bytes 786440 | tf_op jit(solution)/shard_map/ppermute | solution.py:26
  16.7 31.7 %copy-start.3 = (bf16[1,1,4,1024,128]{4,3,2,1,0:T(8,128)(2,1)S(1)}, bf16[1,1,4,1024,128]{4,3,2,1,0:T(8,128)(2,1)}, u32[]{:S(2)}) copy-start(bf16[1,1,4,1024,128]{4,3,2,1,0:T(8,128)(2,1)} %param.33) | copy-start | bytes 3145732
  16.7 3.4 copy-start.58
  24.7 3.4 copy-start.58
  32.6 3.3 copy-start.58
  40.5 3.4 copy-start.58
  144.5 6.3 copy-start.50
  157.6 6.3 copy-start.50
  171.7 6.3 copy-start.50
  185.8 6.3 copy-start.50
  330.9 4.0 copy-start.6
  331.6 737.7 %all-reduce.5.cloned.1.call-start = ((), (), s32[]{:S(2)}) async-start(), calls=%async_computation | async-start | bytes 917504 | tf_op jit(solution)/shard_map/psum | solution.py:11
  333.5 9.9 copy-start.7
  333.5 49.5 %collective-permute-start.5 = (bf16[1024,128]{1,0:T(8,128)(2,1)}, bf16[1024,128]{1,0:T(8,128)(2,1)}, u32[]{:S(2)}, u32[]{:S(2)}) collective-permute-start(bf16[1024,128]{1,0:T(8,128)(2,1)} %convert_element_type.565), channel_id=1, source_target_pairs={{63,0},{0,1},{1,2},{2,3},{3,4},{4,5},{5,6},{6,7},{7,8},{8,9},{9,10... | collective-permute-start | bytes 786440 | tf_op jit(solution)/shard_map/ppermute | solution.py:26
  335.7 47.3 %collective-permute-start.4 = (bf16[1024,128]{1,0:T(8,128)(2,1)}, bf16[1024,128]{1,0:T(8,128)(2,1)}, u32[]{:S(2)}, u32[]{:S(2)}) collective-permute-start(bf16[1024,128]{1,0:T(8,128)(2,1)} %convert_element_type.563), channel_id=1, source_target_pairs={{1,0},{2,1},{3,2},{4,3},{5,4},{6,5},{7,6},{8,7},{9,8},{10,9},{11,1... | collective-permute-start | bytes 786440 | tf_op jit(solution)/shard_map/ppermute | solution.py:26
  343.4 38.4 %copy-start.22 = (bf16[1024,128]{1,0:T(8,128)(2,1)S(1)}, bf16[1024,128]{1,0:T(8,128)(2,1)}, u32[]{:S(2)}) copy-start(bf16[1024,128]{1,0:T(8,128)(2,1)} %get-tuple-element.2003) | copy-start | bytes 786436
  343.4 38.4 %copy-start.23 = (bf16[1024,128]{1,0:T(8,128)(2,1)S(1)}, bf16[1024,128]{1,0:T(8,128)(2,1)}, u32[]{:S(2)}) copy-start(bf16[1024,128]{1,0:T(8,128)(2,1)} %get-tuple-element.2002) | copy-start | bytes 786436
  343.4 38.4 %copy-start.24 = (bf16[1024,128]{1,0:T(8,128)(2,1)S(1)}, bf16[1024,128]{1,0:T(8,128)(2,1)}, u32[]{:S(2)}) copy-start(bf16[1024,128]{1,0:T(8,128)(2,1)} %get-tuple-element.2001) | copy-start | bytes 786436
  344.1 37.7 %copy-start.21 = (bf16[1024,128]{1,0:T(8,128)(2,1)S(1)}, bf16[1024,128]{1,0:T(8,128)(2,1)}, u32[]{:S(2)}) copy-start(bf16[1024,128]{1,0:T(8,128)(2,1)} %get-tuple-element.2004) | copy-start | bytes 786436
  344.1 38.8 %collective-permute-start.3 = (bf16[1024,128]{1,0:T(8,128)(2,1)}, bf16[1024,128]{1,0:T(8,128)(2,1)}, u32[]{:S(2)}, u32[]{:S(2)}) collective-permute-start(bf16[1024,128]{1,0:T(8,128)(2,1)} %convert_element_type.561), channel_id=1, source_target_pairs={{64,0},{128,64},{192,128},{65,1},{129,65},{193,129},{66,2},{130,66... | collective-permute-start | bytes 786440 | tf_op jit(solution)/shard_map/ppermute | solution.py:20
  (199 other events, 228.8 us)
Sparse Core Ops, SparseCore 0:
  331.8 49.9 all-reduce.6
  384.6 684.6 all-reduce.4
